TPU v7x, 128 devices: a whole 4x4x4 slice. The times are simulated.
128 devices in a mesh: fsdp: 32 (over y, z, core), dp: 4 (over x).
Axes of the slice: x: 4, y: 4, z: 4, core: 2. Of those that a mesh axis runs over, the one named last changes fastest.
Arguments:
- tokens: bfloat16 [16384, 4096], P(('fsdp', 'dp')), may hold values from -6 to 6
- gain: float32 [4096], replicated, may hold values from 0.5 to 1.5
- tiles: bfloat16 [512, 128, 128], P('fsdp'), may hold values from -0.25 to 0.25
- tile_rows: int32 [512], replicated, may hold values from 0 to 31, as said below
- tile_cols: int32 [512], replicated, may hold values from 0 to 111, as said below
- cotangent: bfloat16 [16384, 14336], P(('fsdp', 'dp')), may hold values from -6 to 6
Outputs:
- projected: bfloat16 [16384, 14336], P(('fsdp', 'dp'))
- token_grad: bfloat16 [16384, 4096], P(('fsdp', 'dp'))
- tile_grad: float32 [512, 128, 128], P('fsdp')
- gain_grad: float32 [4096], replicated
Inputs may be any that keep to these rules, and one draw needn't show every extreme that they name: The pairs (tile_rows[i], tile_cols[i]) are all different. `tile_cols`: pairs with tile_rows as above.
All inputs are finite; a program needn't handle non-finite values.
Results may differ from a plain program's by a relative error of at most 0.0049.
Values may be sent and summed in bfloat16 or wider, within the bound.
No kernel may reach another device: no remote copies, remote signals or barrier semaphores. Data moves between devices by JAX's collectives and lax.ppermute only.
A program may use at most 256 MiB of HBM per device.

v0:
```python
import jax
import jax.numpy as jnp
from jax import lax
from jax.sharding import PartitionSpec as P


def shards(tokens, gain, tiles, tile_rows, tile_cols, cotangent):
    count = tokens.shape[0]
    width = tokens.shape[1]
    tile = tiles.shape[1]
    row_blocks = width // tile
    col_blocks = cotangent.shape[1] // tile
    x32 = tokens.astype(jnp.float32)
    scale = lax.rsqrt(jnp.mean(x32 * x32, axis=-1, keepdims=True) + 1e-05)
    normed = (x32 * scale * gain).astype(jnp.bfloat16)
    xblocks = normed.reshape(count, row_blocks, tile)
    gblocks = cotangent.reshape(count, col_blocks, tile)
    piece = lax.all_gather(tiles, "fsdp", axis=0, tiled=True)
    rows = tile_rows
    cols = tile_cols
    xsel = jnp.take(xblocks, rows, axis=1)
    gsel = jnp.take(gblocks, cols, axis=1)
    forward = jnp.einsum("tkj,kjm->tkm", xsel, piece, preferred_element_type=jnp.float32)
    backward = jnp.einsum("tkm,kjm->tkj", gsel, piece, preferred_element_type=jnp.float32)
    stacked = jnp.stack([forward, backward], axis=0)
    outsum = jnp.zeros((count, col_blocks, tile), jnp.float32).at[:, tile_cols].add(stacked[0])
    back = jnp.zeros((count, row_blocks, tile), jnp.float32).at[:, tile_rows].add(stacked[1])
    projected = outsum.reshape(count, col_blocks * tile).astype(jnp.bfloat16)
    dnormed = back.reshape(count, width)
    gain_grad = lax.psum(jnp.sum(dnormed * x32 * scale, axis=0), ("fsdp", "dp"))
    inner = jnp.mean(x32 * gain * dnormed, axis=-1, keepdims=True)
    token_grad = (scale * gain * dnormed - x32 * scale**3 * inner).astype(jnp.bfloat16)
    group = tiles.shape[0]
    number = tiles.shape[0] * lax.axis_size("fsdp")

    def group_terms(first):
        rows = lax.dynamic_slice_in_dim(tile_rows, first, group, 0)
        cols = lax.dynamic_slice_in_dim(tile_cols, first, group, 0)
        xsel = jnp.take(xblocks, rows, axis=1)
        gsel = jnp.take(gblocks, cols, axis=1)
        return jnp.einsum("tkj,tkm->kjm", xsel, gsel, preferred_element_type=jnp.float32)

    firsts = group * jnp.arange(number // group, dtype=jnp.int32)
    result = lax.map(group_terms, firsts)
    owned = lax.psum_scatter(
        result.reshape(number, tile, tile), "fsdp", scatter_dimension=0, tiled=True
    )
    tile_grad = lax.psum(owned, "dp")
    return (projected, token_grad, tile_grad, gain_grad)


def solution(mesh):
    placed = (
        P(("fsdp", "dp"), None),
        P(),
        P("fsdp", None, None),
        P(),
        P(),
        P(("fsdp", "dp"), None),
    )
    return jax.shard_map(
        shards,
        mesh=mesh,
        in_specs=placed,
        out_specs=(P(("fsdp", "dp"), None), P(("fsdp", "dp"), None), P("fsdp", None, None), P()),
        check_vma=False,
    )
```

profile of v0, /device:TPU:1, one launch (start us, length us, event | category | flops | bytes accessed | tf_op | source)
XLA Modules:
  0.0 814.4 jit_solution(1176212291491571832)
XLA Ops:
  8.0 6.1 copy.35
  14.0 6.0 copy.36
  21.7 16.2 %gather_fusion.3 = bf16[512,128,128]{2,1,0:T(8,128)(2,1)} fusion(bf16[128,112,128]{2,0,1:T(8,128)(2,1)} %copy.36, s32[1024]{0:T(1024)S(1)} %pad_clamp_fusion.2), kind=kCustom, calls=%fused_computation.3 | custom fusion | bytes 33556480 | tf_op jit(solution)/shard_map/jit(_take)/gather | solution.py:22
  38.5 48.0 %all-gather.2.cloned.1.call-done = bf16[512,128,128]{2,1,0:T(8,128)(2,1)} async-done(((bf16[16,128,128]{2,1,0:T(8,128)(2,1)}), bf16[512,128,128]{2,1,0:T(8,128)(2,1)}) %all-gather.2.cloned.1.call-update) | async-done | bytes 16777232 | tf_op jit(solution)/shard_map/all_gather | solution.py:18
  86.5 28.2 %fusion.9 = f32[512,128,128]{2,1,0:T(8,128)} fusion(bf16[512,128,128]{2,1,0:T(8,128)(2,1)} %all-gather.2.cloned.1.call-done, bf16[512,128,128]{2,1,0:T(8,128)(2,1)} %gather_fusion.3, pred[512]{0:T(512)(128)(4,1)S(1)} %compare_and_fusion.2), kind=kOutput, calls=%fused_computation.22 | convolution fusion | flops 2155872256 | bytes 67109376 | tf_op jit(solution)/shard_map/tkm,kjm->tkj/dot_general | solution.py:24
  115.0 66.1 %scatter_fusion.1 = f32[128,32,128]{2,0,1:T(8,128)S(1)} fusion(f32[128,32,128]{2,0,1:T(8,128)S(1)} %broadcast_in_dim.69, s32[512]{0:T(512)S(1)} %compare_select_fusion.2, f32[512,128,128]{2,1,0:T(8,128)} %fusion.9), kind=kCustom, calls=%fused_computation.5 | custom fusion | flops 8388608 | bytes 100665344 | tf_op jit(solution)/shard_map/scatter-add | solution.py:27
  185.5 2.8 fusion.24
  189.0 237.1 %while.10 = (s32[]{:T(128)}, f32[32,16,128,128]{3,2,1,0:T(8,128)}, s32[32]{0:T(128)S(1)}, s32[512]{0:T(512)S(1)}, bf16[128,32,128]{2,0,1:T(8,128)(2,1)S(1)}, /*i...) while((s32[]{:T(128)}, f32[32,16,128,128]{3,2,1,0:T(8,128)}, ...), condition=%wide.region_5.6_spmd, body=%wide.region_4.5_spmd.sunk | while | flops 67635392 | bytes 4203735 | solution.py:44
  191.6 2.7 gather_fusion
  199.0 2.7 gather_fusion
  206.5 2.7 gather_fusion
  213.9 2.7 gather_fusion
  228.7 2.7 gather_fusion
  250.9 2.7 gather_fusion
  317.6 2.7 gather_fusion
  325.0 2.7 gather_fusion
  347.2 2.7 gather_fusion
  354.6 2.7 gather_fusion
  362.0 2.7 gather_fusion
  376.9 2.7 gather_fusion
  391.7 2.7 gather_fusion
  399.1 2.7 gather_fusion
  421.3 2.7 gather_fusion
  426.4 15.0 %gather_fusion.2 = bf16[512,128,128]{2,1,0:T(8,128)(2,1)} fusion(bf16[128,32,128]{2,0,1:T(8,128)(2,1)S(1)} %get-tuple-element.182, s32[1024]{0:T(1024)S(1)} %pad_clamp_fusion.3), kind=kCustom, calls=%fused_computation.2 | custom fusion | bytes 33556480 | tf_op jit(solution)/shard_map/jit(_take)/gather | solution.py:21
  441.3 148.6 %reduce-scatter.2.cloned.1.call-done = f32[16,128,128]{2,1,0:T(8,128)} async-done(((f32[512,128,128]{2,1,0:T(8,128)}), f32[16,128,128]{2,1,0:T(8,128)}) %reduce-scatter.2.cloned.1.call-update) | async-done | bytes 1048592 | tf_op jit(solution)/shard_map/reduce_scatter | solution.py:45
  590.0 24.5 %fusion.11 = f32[512,128,128]{2,1,0:T(8,128)} fusion(bf16[512,128,128]{2,1,0:T(8,128)(2,1)} %all-gather.2.cloned.1.call-done, bf16[512,128,128]{2,1,0:T(8,128)(2,1)} %gather_fusion.2, pred[512]{0:T(512)(128)(4,1)S(1)} %compare_and_fusion.3), kind=kOutput, calls=%fused_computation.24 | convolution fusion | flops 2155872256 | bytes 67109376 | tf_op jit(solution)/shard_map/tkj,kjm->tkm/dot_general | solution.py:23
  614.5 3.8 broadcast_in_dim.64
  618.3 103.4 %scatter_fusion = f32[128,112,128]{2,0,1:T(8,128)} fusion(f32[128,112,128]{2,0,1:T(8,128)} %broadcast_in_dim.64, s32[512]{0:T(512)S(1)} %compare_select_fusion.3, f32[512,128,128]{2,1,0:T(8,128)} %fusion.11), kind=kCustom, calls=%fused_computation.4 | custom fusion | flops 8388608 | bytes 100665344 | tf_op jit(solution)/shard_map/scatter-add | solution.py:26
  721.7 5.8 convert_element_type.17
  727.5 6.1 copy.34
  733.6 6.1 copy.40
  741.0 64.6 %psum.15 = f32[4096]{0:T(1024)} all-reduce(f32[4096]{0:T(1024)S(1)} %get-tuple-element.68), channel_id=1, replica_groups=mesh['fsdp'=32,'dp'=4] {'fsdp','dp'}, use_global_device_ids=true, to_apply=%region_9.10 | all-reduce | flops 4096 | bytes 32768 | tf_op jit(solution)/shard_map/psum | solution.py:30
  (242 shorter events, 145.7 us)
Async XLA Ops:
  7.2 14.5 %copy-start.2 = (s32[512]{0:T(512)S(1)}, s32[512]{0:T(512)}, u32[]{:S(2)}) copy-start(s32[512]{0:T(512)} %param.12) | copy-start | bytes 6148
  7.2 79.4 %all-gather.2.cloned.1.call-start = ((), (), s32[]{:S(2)}) async-start(), calls=%async_computation.1 | async-start | bytes 17301504 | tf_op jit(solution)/shard_map/all_gather | solution.py:18
  7.9 582.1 %reduce-scatter.2.cloned.1.call-start = ((), (), s32[]{:S(2)}) async-start(), calls=%async_computation.2 | async-start | bytes 34603008 | tf_op jit(solution)/shard_map/reduce_scatter | solution.py:45
  21.7 16.8 %copy-start.3 = (s32[512]{0:T(512)S(1)}, s32[512]{0:T(512)}, u32[]{:S(2)}) copy-start(s32[512]{0:T(512)} %param.11) | copy-start | bytes 6148
  115.0 68.0 %copy-start.1 = (f32[4096]{0:T(1024)S(1)}, f32[4096]{0:T(1024)}, u32[]{:S(2)}) copy-start(f32[4096]{0:T(1024)} %param.9) | copy-start | bytes 49156
  426.1 379.5 %all-reduce.2.cloned.1.call-start = ((), (), s32[]{:S(2)}) async-start(), calls=%async_computation.3 | async-start | bytes 2097152 | tf_op jit(solution)/shard_map/psum | solution.py:48
  721.7 18.0 %copy-start = (bf16[128,4096]{0,1:T(8,128)(2,1)S(1)}, bf16[128,4096]{0,1:T(8,128)(2,1)}, u32[]{:S(2)}) copy-start(bf16[128,4096]{0,1:T(8,128)(2,1)} %get-tuple-element.90) | copy-start | bytes 3145732
Sparse Core Ops, SparseCore 0:
  10.3 76.2 all-gather.1
  426.2 163.6 reduce-scatter.1
  592.5 44.0 all-reduce.1
where the time goes:
time: 820 us; the launch traced here: 814 us
  waiting for transfers between devices  197 us (24%)
  local copies, waits for them, and re-layouts  192 us (23%)
  other arithmetic  184 us (22%)
  matrix products  98.3 us (12%)
  blocking collectives  64.6 us (8%)
  loops' own time  63.1 us (8%)
  between operations  13.9 us (2%)
    reduce_scatter x1, waiting for transfers between devices, shards(): lax.psum_scatter(result.reshape(number, tile, tile), 'fsdp', scatter_dime...  149 us
    scatter-add x1, other arithmetic, shards(): jnp.zeros((count, col_blocks, tile), jnp.float32).at[:, tile_cols]  103 us
    gather x32, local copies, waits for them, and re-layouts, group_terms(): gsel = jnp.take(gblocks, cols, axis=1)  85.9 us
    scatter-add x1, other arithmetic, shards(): jnp.zeros((count, row_blocks, tile), jnp.float32).at[:, tile_rows]  66.1 us
    psum x1, blocking collectives, shards(): gain_grad = lax.psum(jnp.sum(dnormed * x32 * scale, axis=0), ('fsdp', 'dp'))  64.6 us
    another operation x1, loops' own time, shards(): result = lax.map(group_terms, firsts)  63.1 us
    all_gather x1, waiting for transfers between devices, shards(): piece = lax.all_gather(tiles, 'fsdp', axis=0, tiled=True)  48 us
    dot_general x32, matrix products, group_terms(): jnp.einsum('tkj,tkm->kjm', xsel, gsel, preferred_element_type=jnp.float32)  45.6 us
  transfers between devices with their start and end apart: 3, of which 2 were waited for; matrix products, arithmetic and copies ran while one was open for 24% of the time, Pallas kernels for 0%

commit v1 on v0

--- a/solution.py
+++ b/solution.py
@@ -27,7 +27,9 @@
     back = jnp.zeros((count, row_blocks, tile), jnp.float32).at[:, tile_rows].add(stacked[1])
     projected = outsum.reshape(count, col_blocks * tile).astype(jnp.bfloat16)
     dnormed = back.reshape(count, width)
-    gain_grad = lax.psum(jnp.sum(dnormed * x32 * scale, axis=0), ("fsdp", "dp"))
+    gain_grad = lax.psum(
+        lax.psum(jnp.sum(dnormed * x32 * scale, axis=0), axis_name="dp"), axis_name="fsdp"
+    )
     inner = jnp.mean(x32 * gain * dnormed, axis=-1, keepdims=True)
     token_grad = (scale * gain * dnormed - x32 * scale**3 * inner).astype(jnp.bfloat16)
     group = tiles.shape[0]

time: 820 us -> 895 us (1.091)
  blocking collectives: 64.6 us -> 136 us
    psum x1 -> x2, blocking collectives: 64.6 us -> 136 us  [the longest x1 123 us: shards(): lax.psum(lax.psum(jnp.sum(dnormed * x32 * scale, axis=0), axis_name='dp')...]
  transfers between devices with their start and end apart: 3 -> 3, of which waited for: 2 -> 2; matrix products, arithmetic and copies ran while one was open for 24% -> 22% of each run, Pallas kernels for 0% -> 0%
where the time goes in v1:
time: 895 us; the launch traced here: 886 us
  waiting for transfers between devices  197 us (22%)
  local copies, waits for them, and re-layouts  192 us (21%)
  other arithmetic  184 us (21%)
  blocking collectives  136 us (15%)
  matrix products  98.3 us (11%)
  loops' own time  63.1 us (7%)
  between operations  13.9 us (2%)
    reduce_scatter x1, waiting for transfers between devices, shards(): lax.psum_scatter(result.reshape(number, tile, tile), 'fsdp', scatter_dime...  149 us
    psum x1, blocking collectives, shards(): lax.psum(lax.psum(jnp.sum(dnormed * x32 * scale, axis=0), axis_name='dp')...  123 us
    scatter-add x1, other arithmetic, shards(): jnp.zeros((count, col_blocks, tile), jnp.float32).at[:, tile_cols]  103 us
    gather x32, local copies, waits for them, and re-layouts, group_terms(): gsel = jnp.take(gblocks, cols, axis=1)  85.9 us
    scatter-add x1, other arithmetic, shards(): jnp.zeros((count, row_blocks, tile), jnp.float32).at[:, tile_rows]  66.1 us
    another operation x1, loops' own time, shards(): result = lax.map(group_terms, firsts)  63.1 us
    all_gather x1, waiting for transfers between devices, shards(): piece = lax.all_gather(tiles, 'fsdp', axis=0, tiled=True)  48 us
    dot_general x32, matrix products, group_terms(): jnp.einsum('tkj,tkm->kjm', xsel, gsel, preferred_element_type=jnp.float32)  45.6 us
  transfers between devices with their start and end apart: 3, of which 2 were waited for; matrix products, arithmetic and copies ran while one was open for 22% of the time, Pallas kernels for 0%

profile of v1, /device:TPU:1, one launch (start us, length us, event | category | flops | bytes accessed | tf_op | source)
XLA Modules:
  0.0 885.6 jit_solution(10198446258675211272)
XLA Ops:
  8.0 6.1 copy.35
  14.0 6.0 copy.36
  21.7 16.2 %gather_fusion.3 = bf16[512,128,128]{2,1,0:T(8,128)(2,1)} fusion(bf16[128,112,128]{2,0,1:T(8,128)(2,1)} %copy.36, s32[1024]{0:T(1024)S(1)} %pad_clamp_fusion.2), kind=kCustom, calls=%fused_computation.3 | custom fusion | bytes 33556480 | tf_op jit(solution)/shard_map/jit(_take)/gather | solution.py:22
  38.5 48.0 %all-gather.2.cloned.1.call-done = bf16[512,128,128]{2,1,0:T(8,128)(2,1)} async-done(((bf16[16,128,128]{2,1,0:T(8,128)(2,1)}), bf16[512,128,128]{2,1,0:T(8,128)(2,1)}) %all-gather.2.cloned.1.call-update) | async-done | bytes 16777232 | tf_op jit(solution)/shard_map/all_gather | solution.py:18
  86.5 28.2 %fusion.9 = f32[512,128,128]{2,1,0:T(8,128)} fusion(bf16[512,128,128]{2,1,0:T(8,128)(2,1)} %all-gather.2.cloned.1.call-done, bf16[512,128,128]{2,1,0:T(8,128)(2,1)} %gather_fusion.3, pred[512]{0:T(512)(128)(4,1)S(1)} %compare_and_fusion.2), kind=kOutput, calls=%fused_computation.22 | convolution fusion | flops 2155872256 | bytes 67109376 | tf_op jit(solution)/shard_map/tkm,kjm->tkj/dot_general | solution.py:24
  115.0 66.1 %scatter_fusion.1 = f32[128,32,128]{2,0,1:T(8,128)S(1)} fusion(f32[128,32,128]{2,0,1:T(8,128)S(1)} %broadcast_in_dim.69, s32[512]{0:T(512)S(1)} %compare_select_fusion.2, f32[512,128,128]{2,1,0:T(8,128)} %fusion.9), kind=kCustom, calls=%fused_computation.5 | custom fusion | flops 8388608 | bytes 100665344 | tf_op jit(solution)/shard_map/scatter-add | solution.py:27
  185.5 2.8 fusion.24
  189.0 237.1 %while.10 = (s32[]{:T(128)}, f32[32,16,128,128]{3,2,1,0:T(8,128)}, s32[32]{0:T(128)S(1)}, s32[512]{0:T(512)S(1)}, bf16[128,32,128]{2,0,1:T(8,128)(2,1)S(1)}, /*i...) while((s32[]{:T(128)}, f32[32,16,128,128]{3,2,1,0:T(8,128)}, ...), condition=%wide.region_5.6_spmd, body=%wide.region_4.5_spmd.sunk | while | flops 67635392 | bytes 4203735 | solution.py:46
  191.6 2.7 gather_fusion
  199.0 2.7 gather_fusion
  213.9 2.7 gather_fusion
  228.7 2.7 gather_fusion
  250.9 2.7 gather_fusion
  317.6 2.7 gather_fusion
  325.0 2.7 gather_fusion
  347.2 2.7 gather_fusion
  354.6 2.7 gather_fusion
  362.0 2.7 gather_fusion
  376.9 2.7 gather_fusion
  391.7 2.7 gather_fusion
  399.1 2.7 gather_fusion
  421.3 2.7 gather_fusion
  426.4 15.0 %gather_fusion.2 = bf16[512,128,128]{2,1,0:T(8,128)(2,1)} fusion(bf16[128,32,128]{2,0,1:T(8,128)(2,1)S(1)} %get-tuple-element.182, s32[1024]{0:T(1024)S(1)} %pad_clamp_fusion.3), kind=kCustom, calls=%fused_computation.2 | custom fusion | bytes 33556480 | tf_op jit(solution)/shard_map/jit(_take)/gather | solution.py:21
  441.3 148.6 %reduce-scatter.2.cloned.1.call-done = f32[16,128,128]{2,1,0:T(8,128)} async-done(((f32[512,128,128]{2,1,0:T(8,128)}), f32[16,128,128]{2,1,0:T(8,128)}) %reduce-scatter.2.cloned.1.call-update) | async-done | bytes 1048592 | tf_op jit(solution)/shard_map/reduce_scatter | solution.py:47
  590.0 24.5 %fusion.11 = f32[512,128,128]{2,1,0:T(8,128)} fusion(bf16[512,128,128]{2,1,0:T(8,128)(2,1)} %all-gather.2.cloned.1.call-done, bf16[512,128,128]{2,1,0:T(8,128)(2,1)} %gather_fusion.2, pred[512]{0:T(512)(128)(4,1)S(1)} %compare_and_fusion.3), kind=kOutput, calls=%fused_computation.24 | convolution fusion | flops 2155872256 | bytes 67109376 | tf_op jit(solution)/shard_map/tkj,kjm->tkm/dot_general | solution.py:23
  614.5 3.8 broadcast_in_dim.64
  618.3 103.4 %scatter_fusion = f32[128,112,128]{2,0,1:T(8,128)} fusion(f32[128,112,128]{2,0,1:T(8,128)} %broadcast_in_dim.64, s32[512]{0:T(512)S(1)} %compare_select_fusion.3, f32[512,128,128]{2,1,0:T(8,128)} %fusion.11), kind=kCustom, calls=%fused_computation.4 | custom fusion | flops 8388608 | bytes 100665344 | tf_op jit(solution)/shard_map/scatter-add | solution.py:26
  721.7 5.8 convert_element_type.17
  727.5 6.1 copy.34
  733.6 6.1 copy.40
  741.0 12.9 %psum.22 = f32[4096]{0:T(1024)S(1)} all-reduce(f32[4096]{0:T(1024)S(1)} %get-tuple-element.68), channel_id=1, replica_groups=mesh['fsdp'=32,'dp'=4] {'dp'}, use_global_device_ids=true, to_apply=%region_9.10 | all-reduce | flops 4096 | bytes 32768 | tf_op jit(solution)/shard_map/psum | solution.py:31
  753.9 122.9 %psum.23 = f32[4096]{0:T(1024)} all-reduce(f32[4096]{0:T(1024)S(1)} %psum.22), channel_id=1, replica_groups=mesh['fsdp'=32,'dp'=4] {'fsdp'}, use_global_device_ids=true, to_apply=%region_10.11 | all-reduce | flops 4096 | bytes 32768 | tf_op jit(solution)/shard_map/psum | solution.py:30
  (243 shorter events, 148.4 us)
Async XLA Ops:
  7.2 14.5 %copy-start.2 = (s32[512]{0:T(512)S(1)}, s32[512]{0:T(512)}, u32[]{:S(2)}) copy-start(s32[512]{0:T(512)} %param.12) | copy-start | bytes 6148
  7.2 79.4 %all-gather.2.cloned.1.call-start = ((), (), s32[]{:S(2)}) async-start(), calls=%async_computation.1 | async-start | bytes 17301504 | tf_op jit(solution)/shard_map/all_gather | solution.py:18
  7.9 582.1 %reduce-scatter.2.cloned.1.call-start = ((), (), s32[]{:S(2)}) async-start(), calls=%async_computation.2 | async-start | bytes 34603008 | tf_op jit(solution)/shard_map/reduce_scatter | solution.py:47
  21.7 16.8 %copy-start.3 = (s32[512]{0:T(512)S(1)}, s32[512]{0:T(512)}, u32[]{:S(2)}) copy-start(s32[512]{0:T(512)} %param.11) | copy-start | bytes 6148
  115.0 68.0 %copy-start.1 = (f32[4096]{0:T(1024)S(1)}, f32[4096]{0:T(1024)}, u32[]{:S(2)}) copy-start(f32[4096]{0:T(1024)} %param.9) | copy-start | bytes 49156
  426.1 450.7 %all-reduce.2.cloned.1.call-start = ((), (), s32[]{:S(2)}) async-start(), calls=%async_computation.3 | async-start | bytes 2097152 | tf_op jit(solution)/shard_map/psum | solution.py:50
  721.7 18.0 %copy-start = (bf16[128,4096]{0,1:T(8,128)(2,1)S(1)}, bf16[128,4096]{0,1:T(8,128)(2,1)}, u32[]{:S(2)}) copy-start(bf16[128,4096]{0,1:T(8,128)(2,1)} %get-tuple-element.90) | copy-start | bytes 3145732
Sparse Core Ops, SparseCore 0:
  10.3 76.2 all-gather.1
  426.2 163.6 reduce-scatter.1
  592.5 44.0 all-reduce.1
